TPU v7x, 128 devices: a whole 4x4x4 slice. The times are simulated.
128 devices in a mesh: px: 8 (over y, core), py: 16 (over x, z).
Axes of the slice: x: 4, y: 4, z: 4, core: 2. Of those that a mesh axis runs over, the one named last changes fastest.
Arguments:
- parent_field: float32 [192, 384, 640], P('px', 'py'), may hold values from -6 to 6
- nest_field: float32 [192, 384, 640], P('px', 'py'), may hold values from -6 to 6
- anchor: int32 [2], replicated, may hold values from 1 to 125, as said below
- displacement: int32 [2], replicated, may hold values from 1 to 2, as said below
- feedback_weight: float32 [640], replicated, may hold values from 0.3 to 0.9
- rim_weight: float32 [3], replicated, may hold values from 0.3 to 1
Outputs:
- parent_new: float32 [192, 384, 640], P('px', 'py')
- nest_new: float32 [192, 384, 640], P('px', 'py')
Inputs may be any that keep to these rules, and one draw needn't show every extreme that they name: `displacement`: at least one of the two entries equals 2. `anchor`: the two entries differ; one of them equals the largest value.
All inputs are finite; a program needn't handle non-finite values.
Results may differ from a plain program's by a relative error of at most 0.000067.
Values sent between devices are 32-bit elements; how exact they have to be, the bound alone decides.
A program may use at most 128 MiB of HBM per device.

v0:
```python
import jax
import jax.numpy as jnp
from jax import lax
from jax.sharding import PartitionSpec as P

REFINE = 3
MAX_MOVE = 2
RIM_CELLS = 3


def from_behind(value, axis, steps):
    count = lax.axis_size(axis)
    leading, last = (max(0, -steps), min(count, count - steps))
    return lax.ppermute(value, axis, [(source, source + steps) for source in range(leading, last)])


def interp_matrix(rows_total, window_rows):
    row_ids = jnp.arange(rows_total)
    coarse = (row_ids // REFINE)[:, None]
    frac = ((row_ids % REFINE).astype(jnp.float32) + 0.5) / REFINE - 0.5
    frac = frac[:, None]
    columns = jnp.arange(window_rows)[None, :]
    low_side = frac < 0
    weight_left = jnp.where(low_side, -frac, 0.0)
    weight_mid = jnp.where(low_side, 1.0 + frac, 1.0 - frac)
    weight_right = jnp.where(low_side, 0.0, frac)
    result = jnp.where(columns == coarse, weight_left, 0.0)
    result = result + jnp.where(columns == coarse + 1, weight_mid, 0.0)
    result = result + jnp.where(columns == coarse + 2, weight_right, 0.0)
    return result


def rim_blend(distance, rim_weight):
    blend = jnp.zeros(distance.shape, jnp.float32)
    for level in range(RIM_CELLS):
        blend = blend + jnp.where(distance == level, rim_weight[level], 0.0)
    return blend


def local(parent_field, nest_field, anchor, displacement, feedback_weight, rim_weight):
    par_rows, par_cols, chan = parent_field.shape
    nest_rows = nest_field.shape[0]
    nest_cols = nest_field.shape[1]
    count_x = lax.axis_size("px")
    count_y = lax.axis_size("py")
    index_x = lax.axis_index("px")
    index_y = lax.axis_index("py")
    block_x = nest_rows // REFINE
    block_y = nest_cols // REFINE
    window_x = block_x + 2
    window_y = block_y + 2
    shift_x = displacement[0]
    shift_y = displacement[1]
    corner_x = anchor[0] + shift_x
    corner_y = anchor[1] + shift_y
    wanted = jnp.arange(window_x * lax.axis_size("px"))
    global_row = corner_x - 1 + block_x * (wanted // window_x) + wanted % window_x
    local_row = global_row - par_rows * index_x
    inside = (local_row >= 0) & (local_row < par_rows)
    picked = jnp.take(parent_field, jnp.clip(local_row, 0, par_rows - 1), axis=0)
    band = lax.psum_scatter(
        jnp.where(inside[:, None, None], picked, 0.0), "px", scatter_dimension=0, tiled=True
    )
    wanted = jnp.arange(window_y * lax.axis_size("py"))
    global_col = corner_y - 1 + block_y * (wanted // window_y) + wanted % window_y
    local_col = global_col - par_cols * index_y
    inside = (local_col >= 0) & (local_col < par_cols)
    picked = jnp.take(band, jnp.clip(local_col, 0, par_cols - 1), axis=1)
    picked = jnp.where(inside[None, :, None], picked, 0.0)
    window = lax.psum_scatter(jnp.swapaxes(picked, 0, 1), "py", scatter_dimension=0, tiled=True)
    weights_x = interp_matrix(nest_rows, window_x)
    weights_y = interp_matrix(nest_cols, window_y)
    inner_sum = jnp.einsum("jy,yxc->xjc", weights_y, window, precision=lax.Precision.HIGHEST)
    interp = jnp.einsum("ix,xjc->ijc", weights_x, inner_sum, precision=lax.Precision.HIGHEST)
    margin = REFINE * MAX_MOVE
    below = from_behind(nest_field[:margin], "px", -1)
    taller = jnp.concatenate([nest_field, below], axis=0)
    beside = from_behind(taller[:, :margin], "py", -1)
    wider = jnp.concatenate([taller, beside], axis=1)
    shifted = lax.dynamic_slice(
        wider, (REFINE * shift_x, REFINE * shift_y, jnp.int32(0)), nest_field.shape
    )
    nest_nx = nest_rows * count_x
    nest_ny = nest_cols * count_y
    rows_global = nest_rows * index_x + jnp.arange(nest_rows)[:, None, None]
    cols_global = nest_cols * index_y + jnp.arange(nest_cols)[None, :, None]
    newly_entered = (rows_global + REFINE * shift_x >= nest_nx) | (
        cols_global + REFINE * shift_y >= nest_ny
    )
    moved = jnp.where(newly_entered, interp, shifted)
    distance = jnp.minimum(
        jnp.minimum(rows_global, cols_global),
        jnp.minimum(nest_nx - 1 - rows_global, nest_ny - 1 - cols_global),
    )
    blend = rim_blend(distance, rim_weight)
    nest_new = moved + blend * (interp - moved)
    average = nest_new.reshape(block_x, REFINE, block_y, REFINE, chan).sum(axis=(1, 3)) * (
        1.0 / (REFINE * REFINE)
    )
    relative_x = par_rows * index_x + jnp.arange(par_rows) - corner_x
    relative_y = par_cols * index_y + jnp.arange(par_cols) - corner_y
    within_x = (relative_x >= 0) & (relative_x < block_x * count_x)
    within_y = (relative_y >= 0) & (relative_y < block_y * count_y)
    source_x = relative_x // block_x
    source_y = relative_y // block_y
    offset_x = relative_x % block_x
    offset_y = relative_y % block_y
    shards = lax.all_gather(average[None], ("px", "py"), axis=0, tiled=True)
    members = shards.shape[0]
    member = source_x[:, None] * count_y + source_y[None, :]
    valid = within_x[:, None] & within_y[None, :] & (member >= 0) & (member < members)
    flat_index = (
        jnp.clip(member, 0, members - 1) * (block_x * block_y)
        + offset_x[:, None] * block_y
        + offset_y[None, :]
    )
    flat_rows = shards.reshape(members * block_x * block_y, chan)
    picked = jnp.take(flat_rows, flat_index.reshape(-1), axis=0).reshape(par_rows, par_cols, chan)
    summed = jnp.where(valid[:, :, None], picked, 0.0)
    covered = (within_x[:, None] & within_y[None, :])[:, :, None]
    parent_new = jnp.where(
        covered, parent_field + feedback_weight * (summed - parent_field), parent_field
    )
    return (parent_new, nest_new)


def solution(mesh):
    in_specs = (P("px", "py", None), P("px", "py", None), P(), P(), P(), P())
    out_specs = (P("px", "py", None), P("px", "py", None))
    return jax.shard_map(local, mesh=mesh, in_specs=in_specs, out_specs=out_specs, check_vma=False)
```

profile of v0, /device:TPU:1, one launch (start us, length us, event | category | flops | bytes accessed | tf_op | source)
XLA Modules:
  0.0 271.6 jit_solution(3452023540534348857)
XLA Ops:
  7.2 0.0 reduce-scatter.3.cloned.1.call-start
  7.2 1.3 fusion.59
  8.5 1.3 fusion.58
  11.3 4.5 %gather_fusion = f32[80,24,640]{2,1,0:T(8,128)} fusion(f32[24,24,640]{2,1,0:T(8,128)} %param.6, s32[1024]{0:T(1024)S(1)} %pad_clamp_fusion.2), kind=kCustom, calls=%fused_computation | custom fusion | bytes 9830720 | tf_op jit(solution)/shard_map/jit(_take)/gather | solution.py:60
  15.7 5.2 %select_select_fusion.1 = f32[80,24,640]{2,1,0:T(8,128)} fusion(f32[80,24,640]{2,1,0:T(8,128)} %gather_fusion, pred[80]{0:T(512)(128)(4,1)S(1)} %get-tuple-element.20, pred[80]{0:T(512)(128)(4,1)S(1)} %get-tuple-element.21), kind=kLoop, calls=%fused_computation.4 | loop fusion | flops 2457600 | bytes 9830560 | tf_op jit(solution)/shard_map/jit(_where)/select_n | solution.py:62
  20.9 0.0 reduce-scatter.3.cloned.1.call-update
  20.9 0.0 reduce-scatter.5.cloned.1.call-start
  22.3 38.7 %reduce-scatter.3.cloned.1.call-done = f32[10,24,640]{2,1,0:T(8,128)} async-done(((f32[80,24,640]{2,1,0:T(8,128)}), f32[10,24,640]{2,1,0:T(8,128)}) %reduce-scatter.3.cloned.1.call-update) | async-done | bytes 614416 | tf_op jit(solution)/shard_map/reduce_scatter | solution.py:61
  61.0 1.2 copy.27
  62.2 3.7 %gather_fusion.1 = f32[160,10,640]{2,1,0:T(8,128)} fusion(f32[10,24,640]{2,0,1:T(8,128)S(1)} %copy.27, s32[1024]{0:T(1024)S(1)} %pad_clamp_fusion.1), kind=kCustom, calls=%fused_computation.1 | custom fusion | bytes 8192640 | tf_op jit(solution)/shard_map/jit(_take)/gather | solution.py:68
  65.9 5.3 %select_select_fusion = f32[160,10,640]{2,1,0:T(8,128)} fusion(f32[160,10,640]{2,1,0:T(8,128)} %gather_fusion.1, pred[160]{0:T(512)(128)(4,1)S(1)} %get-tuple-element.33, pred[160]{0:T(512)(128)(4,1)S(1)} %get-tuple-element.32), kind=kLoop, calls=%fused_computation.3 | loop fusion | flops 2048000 | bytes 8192320 | tf_op jit(solution)/shard_map/jit(_where)/select_n | solution.py:69
  71.2 0.0 slice-start
  71.2 0.0 copy-start.2
  71.2 0.0 reduce-scatter.5.cloned.1.call-update
  71.2 0.0 all-gather.3.cloned.1.call-start
  71.3 0.9 slice-done
  72.2 0.1 copy.40
  72.3 5.3 %collective-permute-start = (f32[6,24,640]{2,0,1:T(8,128)S(1)}, f32[6,24,640]{2,0,1:T(8,128)S(1)}, u32[]{:S(2)}, u32[]{:S(2)}) collective-permute-start(f32[6,24,640]{2,0,1:T(8,128)S(1)} %copy.40), channel_id=1, source_target_pairs={{16,0},{32,16},{48,32},{64,48},{80,64},{96,80},{112,96},{17,1},{33... | collective-permute-start | bytes 1105928 | tf_op jit(solution)/shard_map/ppermute | solution.py:14
  78.9 0.0 copy-done.2
  78.9 0.7 fusion.57
  79.6 2.0 select_add_fusion
  81.6 0.1 copy.32
  81.7 1.8 constant_dynamic-update-slice_fusion.1
  83.5 0.0 collective-permute-done
  83.7 1.3 collective-permute-start.1
  85.0 0.1 broadcast_or_fusion
  85.0 72.3 %reduce-scatter.5.cloned.1.call-done = f32[10,10,640]{2,1,0:T(8,128)} async-done(((f32[160,10,640]{2,1,0:T(8,128)}), f32[10,10,640]{2,1,0:T(8,128)}) %reduce-scatter.5.cloned.1.call-update) | async-done | bytes 256016 | tf_op jit(solution)/shard_map/reduce_scatter | solution.py:70
  157.3 1.7 convolution_bitcast_fusion
  159.0 0.0 collective-permute-done.1
  159.0 1.9 multiply_add_fusion
  161.0 0.3 copy.33
  161.3 0.0 copy-start.1
  161.3 0.7 reshape.659
  162.0 0.4 copy-done.1
  162.4 1.3 reduce_sum.9
  163.7 1.6 broadcast_multiply_fusion
  165.3 0.0 all-gather.3.cloned.1.call-update
  165.4 0.1 fusion.6
  165.4 0.1 reshape.661
  165.6 0.1 broadcast_and_fusion
  165.7 87.6 %all-gather.3.cloned.1.call-done = f32[1024,8,640]{2,1,0:T(8,128)} async-done(((f32[8,8,640]{2,1,0:T(8,128)}), f32[1024,8,640]{2,1,0:T(8,128)}) %all-gather.3.cloned.1.call-update) | async-done | bytes 20971536 | tf_op jit(solution)/shard_map/all_gather | solution.py:108
  253.3 0.0 copy-start
  253.3 0.0 copy-start.3
  253.3 10.1 %gather_fusion.2 = f32[576,640]{1,0:T(8,128)S(1)} fusion(f32[8192,640]{1,0:T(8,128)} %bitcast.19, s32[1024]{0:T(1024)S(1)} %pad_clamp_fusion), kind=kCustom, calls=%fused_computation.2 | custom fusion | bytes 2951424 | tf_op jit(solution)/shard_map/jit(_take)/gather | solution.py:118
  263.5 0.0 copy-done
  263.5 0.0 copy-done.3
  263.5 1.5 add_select_fusion
  (21 shorter events, 0.3 us)
Async XLA Ops:
  7.2 53.8 %reduce-scatter.3.cloned.1.call-start = ((), (), s32[]{:S(2)}) async-start(), calls=%async_computation.2 | async-start | bytes 5529600 | tf_op jit(solution)/shard_map/reduce_scatter | solution.py:61
  20.9 136.4 %reduce-scatter.5.cloned.1.call-start = ((), (), s32[]{:S(2)}) async-start(), calls=%async_computation.3 | async-start | bytes 6963200 | tf_op jit(solution)/shard_map/reduce_scatter | solution.py:70
  71.2 1.0 slice-start
  71.2 7.7 %copy-start.2 = (f32[3]{0:T(128)S(1)}, f32[3]{0:T(128)}, u32[]{:S(2)}) copy-start(f32[3]{0:T(128)} %param.11) | copy-start | bytes 40
  71.2 182.1 %all-gather.3.cloned.1.call-start = ((), (), s32[]{:S(2)}) async-start(), calls=%async_computation.4 | async-start | bytes 21135360 | tf_op jit(solution)/shard_map/all_gather | solution.py:108
  72.3 11.3 %collective-permute-start = (f32[6,24,640]{2,0,1:T(8,128)S(1)}, f32[6,24,640]{2,0,1:T(8,128)S(1)}, u32[]{:S(2)}, u32[]{:S(2)}) collective-permute-start(f32[6,24,640]{2,0,1:T(8,128)S(1)} %copy.40), channel_id=1, source_target_pairs={{16,0},{32,16},{48,32},{64,48},{80,64},{96,80},{112,96},{17,1},{33... | collective-permute-start | bytes 1105928 | tf_op jit(solution)/shard_map/ppermute | solution.py:14
  83.7 75.3 %collective-permute-start.1 = (f32[30,6,640]{2,0,1:T(8,128)S(1)}, f32[30,6,640]{2,0,1:T(8,128)S(1)}, u32[]{:S(2)}, u32[]{:S(2)}) collective-permute-start(f32[30,6,640]{2,0,1:T(8,128)S(1)} %slice.43), channel_id=1, source_target_pairs={{1,0},{2,1},{3,2},{4,3},{5,4},{6,5},{7,6},{8,7},{9,8},{10,9},{11,1... | collective-permute-start | bytes 1382408 | tf_op jit(solution)/shard_map/ppermute | solution.py:14
  161.3 1.1 copy-start.1
  253.3 10.2 %copy-start = (f32[24,24,640]{2,1,0:T(8,128)S(1)}, f32[24,24,640]{2,1,0:T(8,128)}, u32[]{:S(2)}) copy-start(f32[24,24,640]{2,1,0:T(8,128)} %param.6) | copy-start | bytes 4423684
  253.3 10.2 %copy-start.3 = (f32[640]{0:T(1024)S(1)}, f32[640]{0:T(1024)}, u32[]{:S(2)}) copy-start(f32[640]{0:T(1024)} %param.10) | copy-start | bytes 7684
Sparse Core Ops, SparseCore 0:
  21.0 39.9 reduce-scatter.2
  71.3 85.9 reduce-scatter.4
  165.5 87.8 all-gather.2
where the time goes:
time: 272 us
  waiting for transfers between devices  199 us (73%)
  local copies, waits for them, and re-layouts  27.3 us (10%)
  between operations  17.9 us (7%)
  other arithmetic  17.4 us (6%)
  starting transfers between devices  6.69 us (2%)
  matrix products  3.63 us (1%)
    all_gather x1, waiting for transfers between devices, local(): shards = lax.all_gather(average[None], ('px', 'py'), axis=0, tiled=True)  87.6 us
    reduce_scatter x1, waiting for transfers between devices, local(): lax.psum_scatter(jnp.swapaxes(picked, 0, 1), 'py', scatter_dimension=0, t...  72.3 us
    reduce_scatter x1, waiting for transfers between devices, local(): lax.psum_scatter(jnp.where(inside[:, None, None], picked, 0.0), 'px', sca...  38.7 us
    gather x1, local copies, waits for them, and re-layouts, local(): jnp.take(flat_rows, flat_index.reshape(-1), axis=0)  10.1 us
    ppermute x2, starting transfers between devices, from_behind(): lax.ppermute(value, axis, [(source, source + steps) for source in range(l...  6.57 us
  transfers between devices with their start and end apart: 5, of which 3 were waited for; matrix products, arithmetic and copies ran while one was open for 3% of the time, Pallas kernels for 0%

commit v1 on v0

--- a/solution.py
+++ b/solution.py
@@ -105,7 +105,12 @@
     source_y = relative_y // block_y
     offset_x = relative_x % block_x
     offset_y = relative_y % block_y
-    shards = lax.all_gather(average[None], ("px", "py"), axis=0, tiled=True)
+    shards = jnp.concatenate(
+        lax.all_to_all(
+            jnp.stack([average[None]] * lax.axis_size(("px", "py"))), ("px", "py"), 0, 0
+        ),
+        axis=0,
+    )
     members = shards.shape[0]
     member = source_x[:, None] * count_y + source_y[None, :]
     valid = within_x[:, None] & within_y[None, :] & (member >= 0) & (member < members)

time: 272 us -> 508 us (1.87); the launches traced: 272 us -> 500 us
  waiting for transfers between devices: 199 us -> 408 us
  starting transfers between devices: 6.69 us -> 16.4 us
  local copies, waits for them, and re-layouts: 27.3 us -> 37 us
    all_to_all x0 -> x1, waiting for transfers between devices: none -> 298 us  [local(): lax.all_to_all(jnp.stack([average[None]] * lax.axis_size(('px', 'py'))),...]
    all_gather x1 -> x0, waiting for transfers between devices: 87.6 us -> none  [local(): shards = lax.all_gather(average[None], ('px', 'py'), axis=0, tiled=True)]
    all_to_all x0 -> x1, starting transfers between devices: none -> 9.71 us  [local(): lax.all_to_all(jnp.stack([average[None]] * lax.axis_size(('px', 'py'))),...]
    another operation x0 -> x1, local copies, waits for them, and re-layouts: none -> 9.59 us  [local(): jnp.stack([average[None]] * lax.axis_size(('px', 'py')))]
  transfers between devices with their start and end apart: 5 -> 5, of which waited for: 3 -> 3; matrix products, arithmetic and copies ran while one was open for 3% -> 1% of each run, Pallas kernels for 0% -> 0%
where the time goes in v1:
time: 508 us; the launch traced here: 500 us
  waiting for transfers between devices  408 us (80%)
  local copies, waits for them, and re-layouts  37 us (7%)
  between operations  18.1 us (4%)
  other arithmetic  16.7 us (3%)
  starting transfers between devices  16.4 us (3%)
    all_to_all x1, waiting for transfers between devices, local(): lax.all_to_all(jnp.stack([average[None]] * lax.axis_size(('px', 'py'))),...  298 us
    reduce_scatter x1, waiting for transfers between devices, local(): lax.psum_scatter(jnp.swapaxes(picked, 0, 1), 'py', scatter_dimension=0, t...  72.1 us
    reduce_scatter x1, waiting for transfers between devices, local(): lax.psum_scatter(jnp.where(inside[:, None, None], picked, 0.0), 'px', sca...  38.7 us
  transfers between devices with their start and end apart: 5, of which 3 were waited for; matrix products, arithmetic and copies ran while one was open for 1% of the time, Pallas kernels for 0%

profile of v1, /device:TPU:1, one launch (start us, length us, event | category | flops | bytes accessed | tf_op | source)
XLA Modules:
  0.0 500.2 jit_solution(12691112207759947965)
XLA Ops:
  7.2 0.0 reduce-scatter.3.cloned.1.call-start
  7.2 1.3 fusion.59
  8.5 1.4 fusion.58
  11.2 4.4 gather_fusion
  15.6 5.2 %select_select_fusion.1 = f32[80,24,640]{2,1,0:T(8,128)} fusion(f32[80,24,640]{2,1,0:T(8,128)} %gather_fusion, pred[80]{0:T(512)(128)(4,1)S(1)} %get-tuple-element.20, pred[80]{0:T(512)(128)(4,1)S(1)} %get-tuple-element.21), kind=kLoop, calls=%fused_computation.4 | loop fusion | flops 2457600 | bytes 9830560 | tf_op jit(solution)/shard_map/jit(_where)/select_n | solution.py:62
  20.8 0.0 reduce-scatter.3.cloned.1.call-update
  20.8 0.0 reduce-scatter.5.cloned.1.call-start
  22.2 38.7 %reduce-scatter.3.cloned.1.call-done = f32[10,24,640]{2,1,0:T(8,128)} async-done(((f32[80,24,640]{2,1,0:T(8,128)}), f32[10,24,640]{2,1,0:T(8,128)}) %reduce-scatter.3.cloned.1.call-update) | async-done | bytes 614416 | tf_op jit(solution)/shard_map/reduce_scatter | solution.py:61
  60.9 1.2 copy.27
  62.1 3.7 gather_fusion.1
  65.8 5.3 %select_select_fusion = f32[160,10,640]{2,1,0:T(8,128)} fusion(f32[160,10,640]{2,1,0:T(8,128)} %gather_fusion.1, pred[160]{0:T(512)(128)(4,1)S(1)} %get-tuple-element.33, pred[160]{0:T(512)(128)(4,1)S(1)} %get-tuple-element.32), kind=kLoop, calls=%fused_computation.3 | loop fusion | flops 2048000 | bytes 8192320 | tf_op jit(solution)/shard_map/jit(_where)/select_n | solution.py:69
  71.1 0.0 slice-start
  71.1 0.0 copy-start.2
  71.1 0.0 reduce-scatter.5.cloned.1.call-update
  71.1 1.0 slice-done
  72.1 0.1 copy.40
  72.2 5.3 %collective-permute-start = (f32[6,24,640]{2,0,1:T(8,128)S(1)}, f32[6,24,640]{2,0,1:T(8,128)S(1)}, u32[]{:S(2)}, u32[]{:S(2)}) collective-permute-start(f32[6,24,640]{2,0,1:T(8,128)S(1)} %copy.40), channel_id=1, source_target_pairs={{16,0},{32,16},{48,32},{64,48},{80,64},{96,80},{112,96},{17,1},{33... | collective-permute-start | bytes 1105928 | tf_op jit(solution)/shard_map/ppermute | solution.py:14
  78.8 0.0 copy-done.2
  78.8 0.7 fusion.57
  79.4 2.0 select_add_fusion
  81.4 0.1 copy.32
  81.6 1.8 constant_dynamic-update-slice_fusion.1
  83.4 0.0 collective-permute-done
  83.6 1.3 collective-permute-start.1
  84.9 0.1 broadcast_or_fusion
  84.9 72.1 %reduce-scatter.5.cloned.1.call-done = f32[10,10,640]{2,1,0:T(8,128)} async-done(((f32[160,10,640]{2,1,0:T(8,128)}), f32[10,10,640]{2,1,0:T(8,128)}) %reduce-scatter.5.cloned.1.call-update) | async-done | bytes 256016 | tf_op jit(solution)/shard_map/reduce_scatter | solution.py:70
  157.1 1.7 convolution_bitcast_fusion
  158.8 0.0 collective-permute-done.1
  158.8 1.9 multiply_add_fusion
  160.7 0.3 copy.33
  161.0 0.0 copy-start.1
  161.0 0.7 reshape.653
  161.7 0.4 copy-done.1
  162.1 1.3 reduce_sum.9
  163.5 0.9 broadcast_multiply_fusion
  164.4 9.6 %stack.3 = f32[128,1,8,8,640]{4,3,2,1,0:T(8,128)} broadcast(f32[8,8,640]{2,1,0:T(8,128)S(1)} %broadcast_multiply_fusion), dimensions={2,3,4} | broadcast | bytes 21135360 | tf_op jit(solution)/shard_map/stack | solution.py:110
  174.0 9.7 %all-to-all-start = ((f32[128,1,8,8,640]{4,3,2,1,0:T(8,128)}), f32[128,1,8,8,640]{4,3,2,1,0:T(8,128)}, u32[]{:S(2)}, u32[]{:S(2)}) async-start(f32[128,1,8,8,640]{4,3,2,1,0:T(8,128)} %stack.3), calls=%async_computation.2 | async-start | bytes 41943040 | tf_op jit(solution)/shard_map/all_to_all | solution.py:109
  183.8 0.1 fusion.6
  183.8 0.1 reshape.654
  184.0 0.1 broadcast_and_fusion
  184.1 297.6 %all-to-all-done = f32[128,1,8,8,640]{4,3,2,1,0:T(8,128)} async-done(((f32[128,1,8,8,640]{4,3,2,1,0:T(8,128)}), f32[128,1,8,8,640]{4,3,2,1,0:T(8,128)}, u32[]{:S(2)}, u32[]{:S(2)}) %all-to-all-start) | async-done | bytes 20971552 | tf_op jit(solution)/shard_map/all_to_all | solution.py:109
  481.7 0.0 copy-start
  481.7 0.0 copy-start.3
  481.7 10.1 %gather_fusion.2 = f32[576,640]{1,0:T(8,128)S(1)} fusion(f32[8192,640]{1,0:T(8,128)} %bitcast.11, s32[1024]{0:T(1024)S(1)} %pad_clamp_fusion), kind=kCustom, calls=%fused_computation.2 | custom fusion | bytes 2951424 | tf_op jit(solution)/shard_map/jit(_take)/gather | solution.py:123
  491.8 0.0 copy-done
  491.8 0.0 copy-done.3
  491.8 1.5 add_select_fusion
  (21 shorter events, 0.3 us)
Async XLA Ops:
  7.2 53.7 %reduce-scatter.3.cloned.1.call-start = ((), (), s32[]{:S(2)}) async-start(), calls=%async_computation.3 | async-start | bytes 5529600 | tf_op jit(solution)/shard_map/reduce_scatter | solution.py:61
  20.8 136.3 %reduce-scatter.5.cloned.1.call-start = ((), (), s32[]{:S(2)}) async-start(), calls=%async_computation.4 | async-start | bytes 6963200 | tf_op jit(solution)/shard_map/reduce_scatter | solution.py:70
  71.1 1.0 slice-start
  71.1 7.7 %copy-start.2 = (f32[3]{0:T(128)S(1)}, f32[3]{0:T(128)}, u32[]{:S(2)}) copy-start(f32[3]{0:T(128)} %param.11) | copy-start | bytes 40
  72.2 11.3 %collective-permute-start = (f32[6,24,640]{2,0,1:T(8,128)S(1)}, f32[6,24,640]{2,0,1:T(8,128)S(1)}, u32[]{:S(2)}, u32[]{:S(2)}) collective-permute-start(f32[6,24,640]{2,0,1:T(8,128)S(1)} %copy.40), channel_id=1, source_target_pairs={{16,0},{32,16},{48,32},{64,48},{80,64},{96,80},{112,96},{17,1},{33... | collective-permute-start | bytes 1105928 | tf_op jit(solution)/shard_map/ppermute | solution.py:14
  83.6 75.2 %collective-permute-start.1 = (f32[30,6,640]{2,0,1:T(8,128)S(1)}, f32[30,6,640]{2,0,1:T(8,128)S(1)}, u32[]{:S(2)}, u32[]{:S(2)}) collective-permute-start(f32[30,6,640]{2,0,1:T(8,128)S(1)} %slice.43), channel_id=1, source_target_pairs={{1,0},{2,1},{3,2},{4,3},{5,4},{6,5},{7,6},{8,7},{9,8},{10,9},{11,1... | collective-permute-start | bytes 1382408 | tf_op jit(solution)/shard_map/ppermute | solution.py:14
  161.0 1.1 copy-start.1
  174.0 307.6 %all-to-all-start = ((f32[128,1,8,8,640]{4,3,2,1,0:T(8,128)}), f32[128,1,8,8,640]{4,3,2,1,0:T(8,128)}, u32[]{:S(2)}, u32[]{:S(2)}) async-start(f32[128,1,8,8,640]{4,3,2,1,0:T(8,128)} %stack.3), calls=%async_computation.2 | async-start | bytes 41943040 | tf_op jit(solution)/shard_map/all_to_all | solution.py:109
  481.7 10.2 %copy-start = (f32[24,24,640]{2,1,0:T(8,128)S(1)}, f32[24,24,640]{2,1,0:T(8,128)}, u32[]{:S(2)}) copy-start(f32[24,24,640]{2,1,0:T(8,128)} %param.6) | copy-start | bytes 4423684
  481.7 10.2 %copy-start.3 = (f32[640]{0:T(1024)S(1)}, f32[640]{0:T(1024)}, u32[]{:S(2)}) copy-start(f32[640]{0:T(1024)} %param.10) | copy-start | bytes 7684
Sparse Core Ops, SparseCore 0:
  20.9 39.9 reduce-scatter.2
  71.2 85.7 reduce-scatter.4
